TPU v7x, 32 devices: a whole 2x2x4 slice. The times are simulated.
32 devices in a mesh: pitch: 2 (over core), axial: 4 (over y, x), span: 4 (over z).
Axes of the slice: x: 2, y: 2, z: 4, core: 2. Of those that a mesh axis runs over, the one named last changes fastest.
Arguments:
- state: float32 [5, 16, 128, 512], P(None, 'pitch', 'axial', 'span'), as said below
- coeffs: float32 [2, 4, 5, 128, 512], P(None, None, None, 'axial', 'span'), may hold values from -3 to 3
- lag_shift: int32 [1], replicated, may hold values from 0 to 63
- harmonics: int32 [512], P('span'), may hold values from 1 to 4
Outputs:
- new_state: float32 [5, 16, 128, 512], P(None, 'pitch', 'axial', 'span')
Inputs may be any that keep to these rules, and one draw needn't show every extreme that they name: `state`: density lies in 0.8 to 1.25, momenta within -1.5 to 1.5, total energy within 1.6 to 3.4.
All inputs are finite; a program needn't handle non-finite values.
Results may differ from a plain program's by a relative error of at most 0.0001.
Values sent between devices are 32-bit elements; how exact they have to be, the bound alone decides.
A program may use at most 64 MiB of HBM per device.

v0:
```python
import math
import jax
import jax.numpy as jnp
from jax import lax
from jax.sharding import PartitionSpec as P

HARM_MAX = 4
PERIOD_SAMPLES = 64
HEAT_RATIO_GAS = 1.4
STEP_RATE = 0.25
DAMPING = 0.5
STENCIL = (1.0, -8.0, 28.0, -56.0, 70.0, -56.0, 28.0, -8.0, 1.0)


def padded(cells, sides, width, closed):
    for axis, dim in sides:
        count = lax.axis_size(axis)
        ends = count if closed else count - 1
        head = lax.slice_in_dim(cells, 0, width, axis=dim)
        tail = lax.slice_in_dim(cells, cells.shape[dim] - width, cells.shape[dim], axis=dim)
        cells = jnp.concatenate(
            [
                lax.ppermute(tail, axis, [(i, (i + 1) % count) for i in range(ends)]),
                cells,
                lax.ppermute(head, axis, [((i + 1) % count, i) for i in range(ends)]),
            ],
            axis=dim,
        )
    return cells


def pitch_flux(state):
    density = state[0]
    speed = state[2] / density
    kinetic = 0.5 * (state[1] * state[1] + state[2] * state[2] + state[3] * state[3]) / density
    pressure = (HEAT_RATIO_GAS - 1.0) * (state[4] - kinetic)
    return jnp.stack(
        [
            state[2],
            state[1] * speed,
            state[2] * speed + pressure,
            state[3] * speed,
            (state[4] + pressure) * speed,
        ]
    )


def seam_jump(coeffs, lag_shift, harmonics):
    order = jnp.arange(HARM_MAX)
    phase = (
        2.0
        * math.pi
        / PERIOD_SAMPLES
        * (order + 1).astype(jnp.float32)
        * lag_shift[0].astype(jnp.float32)
    )
    active = (order[:, None] < harmonics[None, :]).astype(jnp.float32)
    cosine = active * jnp.cos(phase)[:, None]
    sine = active * jnp.sin(phase)[:, None]
    first = jnp.sum(cosine[:, None, None, :] * coeffs[0], axis=0)
    second = jnp.sum(sine[:, None, None, :] * coeffs[1], axis=0)
    return first + second


def damping_from(extended, naxial, nspan):
    along = jnp.zeros_like(extended[:, :, 4 : 4 + naxial, 4 : 4 + nspan])
    across = jnp.zeros_like(along)
    for displacement in range(9):
        along = (
            along
            + STENCIL[displacement]
            * extended[:, :, displacement : displacement + naxial, 4 : 4 + nspan]
        )
        across = (
            across
            + STENCIL[displacement]
            * extended[:, :, 4 : 4 + naxial, displacement : displacement + nspan]
        )
    return (along + across) / 256.0


def signed_power(base, count):
    magnitude = jnp.power(jnp.float32(abs(base)), jnp.asarray(count).astype(jnp.float32))
    if base < 0.0:
        magnitude = magnitude * (1 - 2 * (jnp.asarray(count) % 2)).astype(jnp.float32)
    return magnitude


def line_root(main_band_coefficient, neighbour_band_coefficient):
    characteristic_polynomial_radicand = math.sqrt(
        main_band_coefficient * main_band_coefficient
        - 4.0 * neighbour_band_coefficient * neighbour_band_coefficient
    )
    recurrence_decay_number = (-main_band_coefficient + characteristic_polynomial_radicand) / (
        2.0 * neighbour_band_coefficient
    )
    return (
        recurrence_decay_number,
        1.0 / (main_band_coefficient + 2.0 * neighbour_band_coefficient * recurrence_decay_number),
    )


def edge_sums(values, recurrence_decay_number):
    pitch_cells = values.shape[1]
    cell_pos = jnp.arange(pitch_cells)
    tail_part = jnp.einsum(
        "j,fjas->fas",
        signed_power(recurrence_decay_number, pitch_cells - 1 - cell_pos),
        values,
        precision=lax.Precision.HIGHEST,
    )
    head_part = jnp.einsum(
        "j,fjas->fas",
        signed_power(recurrence_decay_number, cell_pos),
        values,
        precision=lax.Precision.HIGHEST,
    )
    return (tail_part, head_part)


def factor_root_weights(step_decays, count):
    return jnp.stack(
        [signed_power(step_decays[0], count), signed_power(step_decays[1], count)], axis=-1
    )


def finish(values, recurrence_decay_number, scale_value, carry_up, carry_down):
    pitch_cells = values.shape[1]
    cell_pos = jnp.arange(pitch_cells)
    kernel = signed_power(recurrence_decay_number, jnp.abs(cell_pos[:, None] - cell_pos[None, :]))
    solved = jnp.einsum("ij,fjas->fias", kernel, values, precision=lax.Precision.HIGHEST)
    enter_weights = signed_power(recurrence_decay_number, cell_pos + 1)
    leave_weights = signed_power(recurrence_decay_number, pitch_cells - cell_pos)
    solved = (
        solved
        + enter_weights[None, :, None, None] * carry_up[:, None]
        + leave_weights[None, :, None, None] * carry_down[:, None]
    )
    return scale_value * solved


def shards(state, coeffs, lag_shift, harmonics):
    flux = pitch_flux(state)
    jump = seam_jump(coeffs, lag_shift, harmonics)
    npitch = lax.axis_size("pitch")
    position = lax.axis_index("pitch")
    at_first = jnp.where(position == 0, 1.0, 0.0).astype(jnp.float32)
    at_last = jnp.where(position == npitch - 1, 1.0, 0.0).astype(jnp.float32)
    widened = padded(flux, (("pitch", 1),), 1, True)
    rhs = 0.75 * (widened[:, 2:] - widened[:, :-2])
    rhs = rhs.at[:, 0].add(0.75 * (at_first * jump))
    rhs = rhs.at[:, -1].add(0.75 * (at_last * jump))
    pitch_cells = rhs.shape[1]
    pitch_total = pitch_cells * npitch
    diffusion = float(pitch_total * pitch_total // 64)
    compact_root, compact_scale = line_root(1.0, 0.25)
    relax_root, relax_scale = line_root(1.0 + 2.0 * diffusion, -diffusion)
    tail_compact, head_compact = edge_sums(rhs, compact_root)
    tail_relax, head_relax = edge_sums(state, relax_root)
    tail_sums = jnp.stack([tail_compact, tail_relax])
    leading_partial_totals = jnp.stack([head_compact, head_relax])
    step_decays = (compact_root**pitch_cells, relax_root**pitch_cells)
    wrap_factors = jnp.array(
        [1.0 / (1.0 - step_decays[0] ** npitch), 1.0 / (1.0 - step_decays[1] ** npitch)],
        jnp.float32,
    )
    collected = (
        lax.all_gather(tail_sums[None], "pitch", axis=0, tiled=True),
        lax.all_gather(leading_partial_totals[None], "pitch", axis=0, tiled=True),
    )
    others = jnp.arange(npitch)
    up_weights = (
        factor_root_weights(step_decays, (position - 1 - others) % npitch) * wrap_factors[None, :]
    )
    descending_sweep_multipliers = (
        factor_root_weights(step_decays, (others - position - 1) % npitch) * wrap_factors[None, :]
    )
    carry_up = jnp.einsum(
        "er,erfas->rfas", up_weights, collected[0], precision=lax.Precision.HIGHEST
    )
    carry_down = jnp.einsum(
        "er,erfas->rfas",
        descending_sweep_multipliers,
        collected[1],
        precision=lax.Precision.HIGHEST,
    )
    deriv = finish(rhs, compact_root, compact_scale, carry_up[0], carry_down[0])
    smoothed_increment = finish(state, relax_root, relax_scale, carry_up[1], carry_down[1])
    extended = padded(state, (("axial", 2), ("span", 3)), 4, False)
    damp = damping_from(extended, state.shape[2], state.shape[3])
    return smoothed_increment - STEP_RATE * deriv - DAMPING * damp


def solution(mesh):
    placed = (
        P(None, "pitch", "axial", "span"),
        P(None, None, None, "axial", "span"),
        P(),
        P("span"),
    )
    return jax.shard_map(
        shards,
        mesh=mesh,
        in_specs=placed,
        out_specs=P(None, "pitch", "axial", "span"),
        check_vma=False,
    )
```

profile of v0, /device:TPU:12, one launch (start us, length us, event | category | flops | bytes accessed | tf_op | source)
XLA Modules:
  0.0 47.0 jit_solution(12623928123771898618)
XLA Ops:
  0.0 1.0 %slice_dynamic-update-slice_fusion = f32[5,8,32,128]{3,2,1,0:T(8,128)S(1)} fusion(f32[5,8,32,128]{3,2,1,0:T(8,128)} %param.9), kind=kLoop, calls=%fused_computation.85 | loop fusion | bytes 262144
  1.0 1.1 %multiply_dynamic-update-slice_fusion.2 = (f32[5,8,32,128]{3,2,1,0:T(8,128)S(1)}, f32[1,8,32,128]{3,2,1,0:T(8,128)S(1)}) fusion(f32[5,8,32,128]{3,2,1,0:T(8,128)S(1)} %slice_dynamic-update-slice_fusion, f32[5,8,32,128]{3,2,1,0:T(8,128)} %param.9), kind=kLoop, calls=%fused_computation.83 | loop fusion | flops 65536 | bytes 655360
  2.9 3.4 %collective-permute-start.2 = (f32[5,8,4,128]{3,1,2,0:T(8,128)S(1)}, f32[5,8,4,128]{3,1,2,0:T(8,128)S(1)}, u32[]{:S(2)}, u32[]{:S(2)}) collective-permute-start(f32[5,8,4,128]{3,1,2,0:T(8,128)S(1)} %copy.68), channel_id=1, source_target_pairs={{0,4},{4,8},{8,12},{1,5},{5,9},{9,13},{2,6},{6,10},{10,14},{3,7},{... | collective-permute-start | bytes 245768 | tf_op jit(solution)/shard_map/ppermute | solution.py:23
  6.3 3.5 %collective-permute-start.3 = (f32[5,8,4,128]{3,1,2,0:T(8,128)S(1)}, f32[5,8,4,128]{3,1,2,0:T(8,128)S(1)}, u32[]{:S(2)}, u32[]{:S(2)}) collective-permute-start(f32[5,8,4,128]{3,1,2,0:T(8,128)S(1)} %copy.69), channel_id=1, source_target_pairs={{4,0},{8,4},{12,8},{5,1},{9,5},{13,9},{6,2},{10,6},{14,10},{7,3},{... | collective-permute-start | bytes 245768 | tf_op jit(solution)/shard_map/ppermute | solution.py:25
  9.8 1.0 %fusion.111 = f32[1,5,32,128]{3,0,2,1:T(1,128)S(1)} fusion(f32[5,8,32,128]{3,2,1,0:T(8,128)S(1)} %copy-done), kind=kOutput, calls=%fused_computation.179 | convolution fusion | flops 1966096 | bytes 737280 | tf_op jit(solution)/shard_map/j,fjas->fas/dot_general | solution.py:106
  10.8 1.0 %fusion.88 = f32[1,5,32,128]{3,0,2,1:T(1,128)S(1)} fusion(f32[5,8,32,128]{3,2,1,0:T(8,128)S(1)} %copy-done), kind=kOutput, calls=%fused_computation.159 | convolution fusion | flops 1966088 | bytes 737280 | tf_op jit(solution)/shard_map/j,fjas->fas/dot_general | solution.py:112
  13.2 1.0 %fusion.41 = f32[1,5,32,128]{3,0,2,1:T(1,128)S(1)} fusion(f32[5,8,32,128]{3,2,1,0:T(8,128)S(1)} %fusion.50), kind=kOutput, calls=%fused_computation.66 | convolution fusion | flops 1966216 | bytes 737280 | tf_op jit(solution)/shard_map/j,fjas->fas/dot_general | solution.py:106
  14.2 1.0 %fusion.39 = f32[1,5,32,128]{3,0,2,1:T(1,128)S(1)} fusion(f32[5,8,32,128]{3,2,1,0:T(8,128)S(1)} %fusion.50), kind=kOutput, calls=%fused_computation.64 | convolution fusion | flops 1966168 | bytes 737280 | tf_op jit(solution)/shard_map/j,fjas->fas/dot_general | solution.py:112
  15.2 2.0 %all-gather = f32[4,5,32,128]{3,2,1,0:T(8,128)S(1)} all-gather(f32[2,5,32,128]{3,2,1,0:T(8,128)S(1)} %pad_maximum_fusion.4), channel_id=2, replica_groups=mesh['pitch'=2,'axial'=4,'span'=4] {'pitch'}, dimensions={0}, use_global_device_ids=true | all-gather | bytes 491520 | tf_op jit(solution)/shard_map/all_gather | solution.py:168
  17.2 2.0 %all-gather.1 = f32[4,5,32,128]{3,2,1,0:T(8,128)S(1)} all-gather(f32[2,5,32,128]{3,2,1,0:T(8,128)S(1)} %pad_maximum_fusion.5), channel_id=3, replica_groups=mesh['pitch'=2,'axial'=4,'span'=4] {'pitch'}, dimensions={0}, use_global_device_ids=true | all-gather | bytes 491520 | tf_op jit(solution)/shard_map/all_gather | solution.py:169
  19.3 1.3 %fusion.48 = f32[2,1,5,32,128]{4,1,3,2,0:T(1,128)S(1)} fusion(f32[2,2,1,1,1]{0,2,4,3,1:T(1,128)S(1)} %copy.37, f32[2,2,5,32,128]{4,3,2,1,0:T(8,128)S(1)} %bitcast.111), kind=kOutput, calls=%fused_computation.75 | convolution fusion | flops 983040 | bytes 491536 | tf_op jit(solution)/shard_map/er,erfas->rfas/dot_general | solution.py:178
  20.6 1.3 %fusion.46 = f32[2,1,5,32,128]{4,1,3,2,0:T(1,128)S(1)} fusion(f32[2,2,1,1,1]{0,2,4,3,1:T(1,128)S(1)} %copy.44, f32[2,2,5,32,128]{4,3,2,1,0:T(8,128)S(1)} %bitcast.112), kind=kOutput, calls=%fused_computation.73 | convolution fusion | flops 983040 | bytes 491536 | tf_op jit(solution)/shard_map/er,erfas->rfas/dot_general | solution.py:181
  21.9 0.6 %constant_dynamic-update-slice_fusion.1 = (f32[5,8,36,128]{3,1,2,0:T(8,128)}, f32[5,8,40,128]{3,1,2,0:T(8,128)S(1)}) fusion(f32[5,8,4,128]{3,1,2,0:T(8,128)S(1)} %collective-permute-done.2), kind=kLoop, calls=%fused_computation.97 | loop fusion | bytes 245760
  22.6 1.6 %constant_dynamic-update-slice_fusion = (f32[5,8,36,128]{3,1,2,0:T(8,128)}, f32[5,8,36,128]{3,1,2,0:T(8,128)}, f32[5,8,40,128]{3,1,2,0:T(8,128)S(1)}) fusion(f32[5,8,36,128]{3,1,2,0:T(8,128)} %get-tuple-element.48, f32[5,8,32,128]{3,2,1,0:T(8,128)S(1)} %copy-done, f32[5,8,40,128]{3,1,2,0:T(8,128)S(1)} %get-tuple-element.49), kind=kLoop, calls=%fused_computation.96 | loop fusion | bytes 2621440 | tf_op jit(solution)/shard_map/concatenate | solution.py:21
  24.2 0.6 %constant_dynamic-update-slice_fusion.2 = (f32[5,8,36,128]{3,1,2,0:T(8,128)}, f32[5,8,40,128]{3,1,2,0:T(8,128)S(1)}) fusion(f32[5,8,36,128]{3,1,2,0:T(8,128)} %get-tuple-element.40, f32[5,8,4,128]{3,1,2,0:T(8,128)S(1)} %collective-permute-done.3, f32[5,8,40,128]{3,1,2,0:T(8,128)S(1)} %get-tuple-element.41), kind=kLoop, calls=%fused_computation.98 | loop fusion | bytes 245760 | tf_op jit(solution)/shard_map/concatenate | solution.py:21
  24.8 1.2 %fusion.152 = (f32[5,8,40,4]{3,1,2,0:T(8,128)}, f32[5,8,40,4]{3,1,2,0:T(8,128)S(1)}) fusion(f32[5,8,40,128]{3,1,2,0:T(8,128)S(1)} %get-tuple-element.51), kind=kLoop, calls=%fused_computation.227 | loop fusion | bytes 102400 | tf_op jit(solution)/shard_map/slice | solution.py:20
  26.0 1.5 %copy.27 = f32[5,8,40,4]{2,1,3,0:T(8,128)S(1)} copy(f32[5,8,40,4]{3,1,2,0:T(8,128)} %get-tuple-element.35) | data formatting | bytes 51200 | tf_op jit(solution)/shard_map/slice | solution.py:20
  27.5 3.5 %collective-permute-start.4 = (f32[5,8,40,4]{2,1,3,0:T(8,128)S(1)}, f32[5,8,40,4]{2,1,3,0:T(8,128)S(1)}, u32[]{:S(2)}, u32[]{:S(2)}) collective-permute-start(f32[5,8,40,4]{2,1,3,0:T(8,128)S(1)} %copy.27), channel_id=1, source_target_pairs={{0,1},{1,2},{2,3},{4,5},{5,6},{6,7},{8,9},{9,10},{10,11},{12,13},{... | collective-permute-start | bytes 76808 | tf_op jit(solution)/shard_map/ppermute | solution.py:23
  31.3 2.5 %collective-permute-start.5 = (f32[5,8,40,4]{2,1,3,0:T(8,128)S(1)}, f32[5,8,40,4]{2,1,3,0:T(8,128)}, u32[]{:S(2)}, u32[]{:S(2)}) collective-permute-start(f32[5,8,40,4]{2,1,3,0:T(8,128)S(1)} %copy.29), channel_id=1, source_target_pairs={{1,0},{2,1},{3,2},{5,4},{6,5},{7,6},{9,8},{10,9},{11,10},{13,12},{... | collective-permute-start | bytes 76808 | tf_op jit(solution)/shard_map/ppermute | solution.py:25
  33.9 2.0 %fusion.6 = f32[5,8,32,128]{3,1,2,0:T(8,128)} fusion(f32[5,8,32,128]{3,2,1,0:T(8,128)S(1)} %fusion.50, f32[5,32,128]{2,1,0:T(8,128)S(1)} %get-tuple-element.47, f32[8]{0:T(128)S(1)} %get-tuple-element.59, f32[5,32,128]{2,1,0:T(8,128)S(1)} %get-tuple-element.45, f32[8]{0:T(128)S(1)} %get-tuple-element.58), kind=kOutput, calls=%fused_computation.20 | convolution fusion | flops 16548992 | bytes 1474624 | tf_op jit(solution)/shard_map/ij,fjas->fias/dot_general | solution.py:131
  36.2 1.5 %collective-permute-done.5 = f32[5,8,40,4]{2,1,3,0:T(8,128)} collective-permute-done((f32[5,8,40,4]{2,1,3,0:T(8,128)S(1)}, f32[5,8,40,4]{2,1,3,0:T(8,128)}, u32[]{:S(2)}, u32[]{:S(2)}) %collective-permute-start.5) | collective-permute-done | bytes 25632 | tf_op jit(solution)/shard_map/ppermute | solution.py:25
  37.8 2.1 %copy.30 = f32[5,8,40,4]{3,1,2,0:T(8,128)} copy(f32[5,8,40,4]{2,1,3,0:T(8,128)} %collective-permute-done.5) | data formatting | bytes 51200 | tf_op jit(solution)/shard_map/ppermute | solution.py:25
  39.9 6.2 %fusion.13 = f32[5,8,32,128]{3,1,2,0:T(8,128)S(1)} fusion(f32[5,8,40,128]{3,1,2,0:T(8,128)S(1)} %get-tuple-element.51, f32[5,8,40,4]{3,1,2,0:T(8,128)} %copy.30, f32[5,8,40,4]{3,1,2,0:T(8,128)S(1)} %copy.28, f32[5,8,36,128]{3,1,2,0:T(8,128)} %get-tuple-element.50, f32[5,8,36,128]{3,1,2,0:T(8,128)} %get-tuple-element.39, ...), kind=kOutput, calls=%fused_computation.27 | convolution fusion | flops 23265472 | bytes 9693184 | tf_op jit(solution)/shard_map/ij,fjas->fias/dot_general | solution.py:131
  46.1 1.0 %copy.31 = f32[5,8,32,128]{3,2,1,0:T(8,128)} copy(f32[5,8,32,128]{3,1,2,0:T(8,128)S(1)} %fusion.13) | data formatting | bytes 1310720 | tf_op jit(solution)/shard_map/sub | solution.py:191
  (43 shorter events, 2.2 us)
Async XLA Ops:
  0.0 2.1 %copy-start = (f32[5,8,32,128]{3,2,1,0:T(8,128)S(1)}, f32[5,8,32,128]{3,2,1,0:T(8,128)}, u32[]{:S(2)}) copy-start(f32[5,8,32,128]{3,2,1,0:T(8,128)} %param.9) | copy-start | bytes 1966084
  2.2 10.7 %collective-permute-start = (f32[5,1,32,128]{3,2,1,0:T(8,128)S(1)}, f32[5,1,32,128]{3,2,1,0:T(8,128)S(1)}, u32[]{:S(2)}, u32[]{:S(2)}) collective-permute-start(f32[5,1,32,128]{3,2,1,0:T(8,128)S(1)} %get-tuple-element.37), channel_id=1, source_target_pairs={{16,0},{0,16},{17,1},{1,17},{18,2},{2,18},{19,3},{3,19},{20,4},{4,... | collective-permute-start | bytes 245768 | tf_op jit(solution)/shard_map/ppermute | solution.py:25
  2.3 10.7 %collective-permute-start.1 = (f32[5,1,32,128]{3,2,1,0:T(8,128)S(1)}, f32[5,1,32,128]{3,2,1,0:T(8,128)S(1)}, u32[]{:S(2)}, u32[]{:S(2)}) collective-permute-start(f32[5,1,32,128]{3,2,1,0:T(8,128)S(1)} %get-tuple-element.38), channel_id=1, source_target_pairs={{0,16},{16,0},{1,17},{17,1},{2,18},{18,2},{3,19},{19,3},{4,20},{20... | collective-permute-start | bytes 245768 | tf_op jit(solution)/shard_map/ppermute | solution.py:23
  2.9 19.0 %collective-permute-start.2 = (f32[5,8,4,128]{3,1,2,0:T(8,128)S(1)}, f32[5,8,4,128]{3,1,2,0:T(8,128)S(1)}, u32[]{:S(2)}, u32[]{:S(2)}) collective-permute-start(f32[5,8,4,128]{3,1,2,0:T(8,128)S(1)} %copy.68), channel_id=1, source_target_pairs={{0,4},{4,8},{8,12},{1,5},{5,9},{9,13},{2,6},{6,10},{10,14},{3,7},{... | collective-permute-start | bytes 245768 | tf_op jit(solution)/shard_map/ppermute | solution.py:23
  6.3 6.3 %copy-start.4 = (f32[2]{0:T(128)S(1)}, f32[2]{0:T(128)}, u32[]{:S(2)}) copy-start(f32[2]{0:T(128)} %constant.173.clone) | copy-start | bytes 28
  6.3 6.5 %copy-start.3 = (s32[128]{0:T(128)S(1)}, s32[128]{0:T(128)}, u32[]{:S(2)}) copy-start(s32[128]{0:T(128)} %param.12) | copy-start | bytes 1540
  6.3 6.6 %copy-start.1 = (f32[2,4,5,32,128]{4,3,2,1,0:T(8,128)S(1)}, f32[2,4,5,32,128]{4,3,2,1,0:T(8,128)}, u32[]{:S(2)}) copy-start(f32[2,4,5,32,128]{4,3,2,1,0:T(8,128)} %param.10) | copy-start | bytes 1966084
  6.3 17.9 %collective-permute-start.3 = (f32[5,8,4,128]{3,1,2,0:T(8,128)S(1)}, f32[5,8,4,128]{3,1,2,0:T(8,128)S(1)}, u32[]{:S(2)}, u32[]{:S(2)}) collective-permute-start(f32[5,8,4,128]{3,1,2,0:T(8,128)S(1)} %copy.69), channel_id=1, source_target_pairs={{4,0},{8,4},{12,8},{5,1},{9,5},{13,9},{6,2},{10,6},{14,10},{7,3},{... | collective-permute-start | bytes 245768 | tf_op jit(solution)/shard_map/ppermute | solution.py:25
  27.5 8.4 %collective-permute-start.4 = (f32[5,8,40,4]{2,1,3,0:T(8,128)S(1)}, f32[5,8,40,4]{2,1,3,0:T(8,128)S(1)}, u32[]{:S(2)}, u32[]{:S(2)}) collective-permute-start(f32[5,8,40,4]{2,1,3,0:T(8,128)S(1)} %copy.27), channel_id=1, source_target_pairs={{0,1},{1,2},{2,3},{4,5},{5,6},{6,7},{8,9},{9,10},{10,11},{12,13},{... | collective-permute-start | bytes 76808 | tf_op jit(solution)/shard_map/ppermute | solution.py:23
  31.3 6.4 %collective-permute-start.5 = (f32[5,8,40,4]{2,1,3,0:T(8,128)S(1)}, f32[5,8,40,4]{2,1,3,0:T(8,128)}, u32[]{:S(2)}, u32[]{:S(2)}) collective-permute-start(f32[5,8,40,4]{2,1,3,0:T(8,128)S(1)} %copy.29), channel_id=1, source_target_pairs={{1,0},{2,1},{3,2},{5,4},{6,5},{7,6},{9,8},{10,9},{11,10},{13,12},{... | collective-permute-start | bytes 76808 | tf_op jit(solution)/shard_map/ppermute | solution.py:25
  35.9 4.0 %copy-start.2 = (f32[5,8,32,128]{3,1,2,0:T(8,128)S(1)}, f32[5,8,32,128]{3,1,2,0:T(8,128)}, u32[]{:S(2)}) copy-start(f32[5,8,32,128]{3,1,2,0:T(8,128)} %fusion.6) | copy-start | bytes 1966084
where the time goes:
time: 47.4 us; the launch traced here: 47 us
  matrix products  14.6 us (31%)
  starting transfers between devices  13.5 us (28%)
  local copies, waits for them, and re-layouts  10.6 us (22%)
  blocking collectives  4.08 us (9%)
  other arithmetic  1.7 us (4%)
  waiting for transfers between devices  1.55 us (3%)
  between operations  0.96 us (2%)
    dot_general x2, matrix products, finish(): jnp.einsum('ij,fjas->fias', kernel, values, precision=lax.Precision.HIGHEST)  8.15 us
    ppermute x3, starting transfers between devices, padded(): lax.ppermute(tail, axis, [(i, (i + 1) % count) for i in range(ends)])  7.38 us
    ppermute x3, starting transfers between devices, padded(): lax.ppermute(head, axis, [((i + 1) % count, i) for i in range(ends)])  6.08 us
    slice x2, local copies, waits for them, and re-layouts, padded(): lax.slice_in_dim(cells, cells.shape[dim] - width, cells.shape[dim], axis=...  2.65 us
    concatenate x2, local copies, waits for them, and re-layouts, padded(): jnp.concatenate([lax.ppermute(tail, axis, [(i, (i + 1) % count) for i in...  2.25 us
    ppermute x1, local copies, waits for them, and re-layouts, padded(): lax.ppermute(head, axis, [((i + 1) % count, i) for i in range(ends)])  2.12 us
    all_gather x1, blocking collectives, shards(): lax.all_gather(tail_sums[None], 'pitch', axis=0, tiled=True)  2.04 us
    all_gather x1, blocking collectives, shards(): lax.all_gather(leading_partial_totals[None], 'pitch', axis=0, tiled=True)  2.04 us
  transfers between devices with their start and end apart: 6, of which 1 were waited for; matrix products, arithmetic and copies ran while one was open for 26% of the time, Pallas kernels for 0%

commit v1 on v0

--- a/solution.py
+++ b/solution.py
@@ -165,7 +165,10 @@
         jnp.float32,
     )
     collected = (
-        lax.all_gather(tail_sums[None], "pitch", axis=0, tiled=True),
+        jnp.concatenate(
+            lax.all_to_all(jnp.stack([tail_sums[None]] * lax.axis_size("pitch")), "pitch", 0, 0),
+            axis=0,
+        ),
         lax.all_gather(leading_partial_totals[None], "pitch", axis=0, tiled=True),
     )
     others = jnp.arange(npitch)

time: 47.4 us -> 49.7 us (1.049)
  starting transfers between devices: 13.5 us -> 16.9 us
  blocking collectives: 4.08 us -> 2.16 us
  other arithmetic: 1.7 us -> 2.46 us
    all_to_all x0 -> x1, starting transfers between devices: none -> 3.46 us  [shards(): lax.all_to_all(jnp.stack([tail_sums[None]] * lax.axis_size('pitch')), 'pi...]
    all_gather x1 -> x0, blocking collectives: 2.04 us -> none  [shards(): lax.all_gather(tail_sums[None], 'pitch', axis=0, tiled=True)]
    another operation x1 -> x2, other arithmetic: 0.01 us -> 0.77 us  [shards(): jnp.stack([tail_sums[None]] * lax.axis_size('pitch'))]
  transfers between devices with their start and end apart: 6 -> 7, of which waited for: 1 -> 1; matrix products, arithmetic and copies ran while one was open for 26% -> 26% of each run, Pallas kernels for 0% -> 0%
where the time goes in v1:
time: 49.7 us; the launch traced here: 49.4 us
  starting transfers between devices  16.9 us (34%)
  matrix products  14.6 us (29%)
  local copies, waits for them, and re-layouts  10.7 us (22%)
  other arithmetic  2.46 us (5%)
  blocking collectives  2.16 us (4%)
  waiting for transfers between devices  1.55 us (3%)
  between operations  0.97 us (2%)
    dot_general x2, matrix products, finish(): jnp.einsum('ij,fjas->fias', kernel, values, precision=lax.Precision.HIGHEST)  8.14 us
    ppermute x3, starting transfers between devices, padded(): lax.ppermute(tail, axis, [(i, (i + 1) % count) for i in range(ends)])  7.38 us
    ppermute x3, starting transfers between devices, padded(): lax.ppermute(head, axis, [((i + 1) % count, i) for i in range(ends)])  6.08 us
    all_to_all x1, starting transfers between devices, shards(): lax.all_to_all(jnp.stack([tail_sums[None]] * lax.axis_size('pitch')), 'pi...  3.46 us
    slice x2, local copies, waits for them, and re-layouts, padded(): lax.slice_in_dim(cells, cells.shape[dim] - width, cells.shape[dim], axis=...  2.66 us
    concatenate x2, local copies, waits for them, and re-layouts, padded(): jnp.concatenate([lax.ppermute(tail, axis, [(i, (i + 1) % count) for i in...  2.23 us
    all_gather x1, blocking collectives, shards(): lax.all_gather(leading_partial_totals[None], 'pitch', axis=0, tiled=True)  2.16 us
    ppermute x1, local copies, waits for them, and re-layouts, padded(): lax.ppermute(head, axis, [((i + 1) % count, i) for i in range(ends)])  2.13 us
  transfers between devices with their start and end apart: 7, of which 1 were waited for; matrix products, arithmetic and copies ran while one was open for 26% of the time, Pallas kernels for 0%

profile of v1, /device:TPU:12, one launch (start us, length us, event | category | flops | bytes accessed | tf_op | source)
XLA Modules:
  0.0 49.4 jit_solution(1108622383612066474)
XLA Ops:
  0.0 1.0 %slice_dynamic-update-slice_fusion = f32[5,8,32,128]{3,2,1,0:T(8,128)S(1)} fusion(f32[5,8,32,128]{3,2,1,0:T(8,128)} %param.9), kind=kLoop, calls=%fused_computation.86 | loop fusion | bytes 262144
  1.0 1.1 %multiply_dynamic-update-slice_fusion.2 = (f32[5,8,32,128]{3,2,1,0:T(8,128)S(1)}, f32[1,8,32,128]{3,2,1,0:T(8,128)S(1)}) fusion(f32[5,8,32,128]{3,2,1,0:T(8,128)S(1)} %slice_dynamic-update-slice_fusion, f32[5,8,32,128]{3,2,1,0:T(8,128)} %param.9), kind=kLoop, calls=%fused_computation.84 | loop fusion | flops 65536 | bytes 655360
  2.9 3.4 %collective-permute-start.2 = (f32[5,8,4,128]{3,1,2,0:T(8,128)S(1)}, f32[5,8,4,128]{3,1,2,0:T(8,128)S(1)}, u32[]{:S(2)}, u32[]{:S(2)}) collective-permute-start(f32[5,8,4,128]{3,1,2,0:T(8,128)S(1)} %copy.68), channel_id=1, source_target_pairs={{0,4},{4,8},{8,12},{1,5},{5,9},{9,13},{2,6},{6,10},{10,14},{3,7},{... | collective-permute-start | bytes 245768 | tf_op jit(solution)/shard_map/ppermute | solution.py:23
  6.3 3.5 %collective-permute-start.3 = (f32[5,8,4,128]{3,1,2,0:T(8,128)S(1)}, f32[5,8,4,128]{3,1,2,0:T(8,128)S(1)}, u32[]{:S(2)}, u32[]{:S(2)}) collective-permute-start(f32[5,8,4,128]{3,1,2,0:T(8,128)S(1)} %copy.69), channel_id=1, source_target_pairs={{4,0},{8,4},{12,8},{5,1},{9,5},{13,9},{6,2},{10,6},{14,10},{7,3},{... | collective-permute-start | bytes 245768 | tf_op jit(solution)/shard_map/ppermute | solution.py:25
  9.8 1.0 %fusion.111 = f32[1,5,32,128]{3,0,2,1:T(1,128)S(1)} fusion(f32[5,8,32,128]{3,2,1,0:T(8,128)S(1)} %copy-done), kind=kOutput, calls=%fused_computation.180 | convolution fusion | flops 1966096 | bytes 737280 | tf_op jit(solution)/shard_map/j,fjas->fas/dot_general | solution.py:106
  10.8 1.0 %fusion.88 = f32[1,5,32,128]{3,0,2,1:T(1,128)S(1)} fusion(f32[5,8,32,128]{3,2,1,0:T(8,128)S(1)} %copy-done), kind=kOutput, calls=%fused_computation.160 | convolution fusion | flops 1966088 | bytes 737280 | tf_op jit(solution)/shard_map/j,fjas->fas/dot_general | solution.py:112
  13.2 1.0 %fusion.41 = f32[1,5,32,128]{3,0,2,1:T(1,128)S(1)} fusion(f32[5,8,32,128]{3,2,1,0:T(8,128)S(1)} %fusion.50), kind=kOutput, calls=%fused_computation.66 | convolution fusion | flops 1966216 | bytes 737280 | tf_op jit(solution)/shard_map/j,fjas->fas/dot_general | solution.py:106
  14.2 1.0 %fusion.39 = f32[1,5,32,128]{3,0,2,1:T(1,128)S(1)} fusion(f32[5,8,32,128]{3,2,1,0:T(8,128)S(1)} %fusion.50), kind=kOutput, calls=%fused_computation.64 | convolution fusion | flops 1966168 | bytes 737280 | tf_op jit(solution)/shard_map/j,fjas->fas/dot_general | solution.py:112
  15.2 0.8 %pad_maximum_fusion.4 = f32[2,1,2,5,32,128]{5,4,3,2,1,0:T(8,128)} fusion(f32[1,1,2,5,32,128]{5,4,3,2,1,0:T(8,128)S(1)} %maximum_bitcast_fusion), kind=kLoop, calls=%fused_computation.69 | loop fusion | flops 81920 | bytes 491520 | tf_op jit(solution)/shard_map/stack | solution.py:169
  15.9 3.5 %all-to-all-start = ((f32[2,1,2,5,32,128]{5,4,3,2,1,0:T(8,128)}), f32[2,1,2,5,32,128]{5,4,3,2,1,0:T(8,128)S(1)}, u32[]{:S(2)}, u32[]{:S(2)}) async-start(f32[2,1,2,5,32,128]{5,4,3,2,1,0:T(8,128)} %pad_maximum_fusion.4), calls=%async_computation | async-start | bytes 655360 | tf_op jit(solution)/shard_map/all_to_all | solution.py:169
  19.4 2.2 %all-gather = f32[4,5,32,128]{3,2,1,0:T(8,128)S(1)} all-gather(f32[2,5,32,128]{3,2,1,0:T(8,128)S(1)} %pad_maximum_fusion.5), channel_id=2, replica_groups=mesh['pitch'=2,'axial'=4,'span'=4] {'pitch'}, dimensions={0}, use_global_device_ids=true | all-gather | bytes 491520 | tf_op jit(solution)/shard_map/all_gather | solution.py:172
  21.6 1.3 %fusion.48 = f32[2,1,5,32,128]{4,1,3,2,0:T(1,128)S(1)} fusion(f32[2,2,1,1,1]{0,2,4,3,1:T(1,128)S(1)} %copy.37, f32[2,2,5,32,128]{4,3,2,1,0:T(8,128)S(1)} %bitcast.113), kind=kOutput, calls=%fused_computation.76 | convolution fusion | flops 983040 | bytes 491536 | tf_op jit(solution)/shard_map/er,erfas->rfas/dot_general | solution.py:181
  22.9 1.3 %fusion.46 = f32[2,1,5,32,128]{4,1,3,2,0:T(1,128)S(1)} fusion(f32[2,2,1,1,1]{0,2,4,3,1:T(1,128)S(1)} %copy.44, f32[2,2,5,32,128]{4,3,2,1,0:T(8,128)S(1)} %bitcast.114), kind=kOutput, calls=%fused_computation.74 | convolution fusion | flops 983040 | bytes 491536 | tf_op jit(solution)/shard_map/er,erfas->rfas/dot_general | solution.py:184
  24.2 0.7 %constant_dynamic-update-slice_fusion.1 = (f32[5,8,36,128]{3,1,2,0:T(8,128)}, f32[5,8,40,128]{3,1,2,0:T(8,128)S(1)}) fusion(f32[5,8,4,128]{3,1,2,0:T(8,128)S(1)} %collective-permute-done.2), kind=kLoop, calls=%fused_computation.98 | loop fusion | bytes 245760
  24.9 1.6 %constant_dynamic-update-slice_fusion = (f32[5,8,36,128]{3,1,2,0:T(8,128)}, f32[5,8,36,128]{3,1,2,0:T(8,128)}, f32[5,8,40,128]{3,1,2,0:T(8,128)S(1)}) fusion(f32[5,8,36,128]{3,1,2,0:T(8,128)} %get-tuple-element.48, f32[5,8,32,128]{3,2,1,0:T(8,128)S(1)} %copy-done, f32[5,8,40,128]{3,1,2,0:T(8,128)S(1)} %get-tuple-element.49), kind=kLoop, calls=%fused_computation.97 | loop fusion | bytes 2621440 | tf_op jit(solution)/shard_map/concatenate | solution.py:21
  27.1 1.2 %fusion.152 = (f32[5,8,40,4]{3,1,2,0:T(8,128)}, f32[5,8,40,4]{3,1,2,0:T(8,128)S(1)}) fusion(f32[5,8,40,128]{3,1,2,0:T(8,128)S(1)} %get-tuple-element.51), kind=kLoop, calls=%fused_computation.228 | loop fusion | bytes 102400 | tf_op jit(solution)/shard_map/slice | solution.py:20
  28.3 1.5 %copy.27 = f32[5,8,40,4]{2,1,3,0:T(8,128)S(1)} copy(f32[5,8,40,4]{3,1,2,0:T(8,128)} %get-tuple-element.35) | data formatting | bytes 51200 | tf_op jit(solution)/shard_map/slice | solution.py:20
  29.8 3.5 %collective-permute-start.4 = (f32[5,8,40,4]{2,1,3,0:T(8,128)S(1)}, f32[5,8,40,4]{2,1,3,0:T(8,128)S(1)}, u32[]{:S(2)}, u32[]{:S(2)}) collective-permute-start(f32[5,8,40,4]{2,1,3,0:T(8,128)S(1)} %copy.27), channel_id=1, source_target_pairs={{0,1},{1,2},{2,3},{4,5},{5,6},{6,7},{8,9},{9,10},{10,11},{12,13},{... | collective-permute-start | bytes 76808 | tf_op jit(solution)/shard_map/ppermute | solution.py:23
  33.6 2.5 %collective-permute-start.5 = (f32[5,8,40,4]{2,1,3,0:T(8,128)S(1)}, f32[5,8,40,4]{2,1,3,0:T(8,128)}, u32[]{:S(2)}, u32[]{:S(2)}) collective-permute-start(f32[5,8,40,4]{2,1,3,0:T(8,128)S(1)} %copy.29), channel_id=1, source_target_pairs={{1,0},{2,1},{3,2},{5,4},{6,5},{7,6},{9,8},{10,9},{11,10},{13,12},{... | collective-permute-start | bytes 76808 | tf_op jit(solution)/shard_map/ppermute | solution.py:25
  36.2 2.0 %fusion.6 = f32[5,8,32,128]{3,1,2,0:T(8,128)} fusion(f32[5,8,32,128]{3,2,1,0:T(8,128)S(1)} %fusion.50, f32[5,32,128]{2,1,0:T(8,128)S(1)} %get-tuple-element.47, f32[8]{0:T(128)S(1)} %get-tuple-element.59, f32[5,32,128]{2,1,0:T(8,128)S(1)} %get-tuple-element.45, f32[8]{0:T(128)S(1)} %get-tuple-element.58), kind=kOutput, calls=%fused_computation.20 | convolution fusion | flops 16548992 | bytes 1474624 | tf_op jit(solution)/shard_map/ij,fjas->fias/dot_general | solution.py:131
  38.6 1.5 %collective-permute-done.5 = f32[5,8,40,4]{2,1,3,0:T(8,128)} collective-permute-done((f32[5,8,40,4]{2,1,3,0:T(8,128)S(1)}, f32[5,8,40,4]{2,1,3,0:T(8,128)}, u32[]{:S(2)}, u32[]{:S(2)}) %collective-permute-start.5) | collective-permute-done | bytes 25632 | tf_op jit(solution)/shard_map/ppermute | solution.py:25
  40.1 2.1 %copy.30 = f32[5,8,40,4]{3,1,2,0:T(8,128)} copy(f32[5,8,40,4]{2,1,3,0:T(8,128)} %collective-permute-done.5) | data formatting | bytes 51200 | tf_op jit(solution)/shard_map/ppermute | solution.py:25
  42.2 6.2 %fusion.13 = f32[5,8,32,128]{3,1,2,0:T(8,128)S(1)} fusion(f32[5,8,40,128]{3,1,2,0:T(8,128)S(1)} %get-tuple-element.51, f32[5,8,40,4]{3,1,2,0:T(8,128)} %copy.30, f32[5,8,40,4]{3,1,2,0:T(8,128)S(1)} %copy.28, f32[5,8,36,128]{3,1,2,0:T(8,128)} %get-tuple-element.50, f32[5,8,36,128]{3,1,2,0:T(8,128)} %get-tuple-element.39, ...), kind=kOutput, calls=%fused_computation.27 | convolution fusion | flops 23265472 | bytes 9693184 | tf_op jit(solution)/shard_map/ij,fjas->fias/dot_general | solution.py:131
  48.4 1.0 %copy.31 = f32[5,8,32,128]{3,2,1,0:T(8,128)} copy(f32[5,8,32,128]{3,1,2,0:T(8,128)S(1)} %fusion.13) | data formatting | bytes 1310720 | tf_op jit(solution)/shard_map/sub | solution.py:194
  (45 shorter events, 2.9 us)
Async XLA Ops:
  0.0 2.1 %copy-start = (f32[5,8,32,128]{3,2,1,0:T(8,128)S(1)}, f32[5,8,32,128]{3,2,1,0:T(8,128)}, u32[]{:S(2)}) copy-start(f32[5,8,32,128]{3,2,1,0:T(8,128)} %param.9) | copy-start | bytes 1966084
  2.2 10.7 %collective-permute-start = (f32[5,1,32,128]{3,2,1,0:T(8,128)S(1)}, f32[5,1,32,128]{3,2,1,0:T(8,128)S(1)}, u32[]{:S(2)}, u32[]{:S(2)}) collective-permute-start(f32[5,1,32,128]{3,2,1,0:T(8,128)S(1)} %get-tuple-element.37), channel_id=1, source_target_pairs={{16,0},{0,16},{17,1},{1,17},{18,2},{2,18},{19,3},{3,19},{20,4},{4,... | collective-permute-start | bytes 245768 | tf_op jit(solution)/shard_map/ppermute | solution.py:25
  2.3 10.7 %collective-permute-start.1 = (f32[5,1,32,128]{3,2,1,0:T(8,128)S(1)}, f32[5,1,32,128]{3,2,1,0:T(8,128)S(1)}, u32[]{:S(2)}, u32[]{:S(2)}) collective-permute-start(f32[5,1,32,128]{3,2,1,0:T(8,128)S(1)} %get-tuple-element.38), channel_id=1, source_target_pairs={{0,16},{16,0},{1,17},{17,1},{2,18},{18,2},{3,19},{19,3},{4,20},{20... | collective-permute-start | bytes 245768 | tf_op jit(solution)/shard_map/ppermute | solution.py:23
  2.9 21.4 %collective-permute-start.2 = (f32[5,8,4,128]{3,1,2,0:T(8,128)S(1)}, f32[5,8,4,128]{3,1,2,0:T(8,128)S(1)}, u32[]{:S(2)}, u32[]{:S(2)}) collective-permute-start(f32[5,8,4,128]{3,1,2,0:T(8,128)S(1)} %copy.68), channel_id=1, source_target_pairs={{0,4},{4,8},{8,12},{1,5},{5,9},{9,13},{2,6},{6,10},{10,14},{3,7},{... | collective-permute-start | bytes 245768 | tf_op jit(solution)/shard_map/ppermute | solution.py:23
  6.3 6.3 %copy-start.4 = (f32[2]{0:T(128)S(1)}, f32[2]{0:T(128)}, u32[]{:S(2)}) copy-start(f32[2]{0:T(128)} %constant.173.clone) | copy-start | bytes 28
  6.3 6.5 %copy-start.3 = (s32[128]{0:T(128)S(1)}, s32[128]{0:T(128)}, u32[]{:S(2)}) copy-start(s32[128]{0:T(128)} %param.12) | copy-start | bytes 1540
  6.3 6.6 %copy-start.1 = (f32[2,4,5,32,128]{4,3,2,1,0:T(8,128)S(1)}, f32[2,4,5,32,128]{4,3,2,1,0:T(8,128)}, u32[]{:S(2)}) copy-start(f32[2,4,5,32,128]{4,3,2,1,0:T(8,128)} %param.10) | copy-start | bytes 1966084
  6.3 20.2 %collective-permute-start.3 = (f32[5,8,4,128]{3,1,2,0:T(8,128)S(1)}, f32[5,8,4,128]{3,1,2,0:T(8,128)S(1)}, u32[]{:S(2)}, u32[]{:S(2)}) collective-permute-start(f32[5,8,4,128]{3,1,2,0:T(8,128)S(1)} %copy.69), channel_id=1, source_target_pairs={{4,0},{8,4},{12,8},{5,1},{9,5},{13,9},{6,2},{10,6},{14,10},{7,3},{... | collective-permute-start | bytes 245768 | tf_op jit(solution)/shard_map/ppermute | solution.py:25
  15.9 5.6 %all-to-all-start = ((f32[2,1,2,5,32,128]{5,4,3,2,1,0:T(8,128)}), f32[2,1,2,5,32,128]{5,4,3,2,1,0:T(8,128)S(1)}, u32[]{:S(2)}, u32[]{:S(2)}) async-start(f32[2,1,2,5,32,128]{5,4,3,2,1,0:T(8,128)} %pad_maximum_fusion.4), calls=%async_computation | async-start | bytes 655360 | tf_op jit(solution)/shard_map/all_to_all | solution.py:169
  29.8 8.4 %collective-permute-start.4 = (f32[5,8,40,4]{2,1,3,0:T(8,128)S(1)}, f32[5,8,40,4]{2,1,3,0:T(8,128)S(1)}, u32[]{:S(2)}, u32[]{:S(2)}) collective-permute-start(f32[5,8,40,4]{2,1,3,0:T(8,128)S(1)} %copy.27), channel_id=1, source_target_pairs={{0,1},{1,2},{2,3},{4,5},{5,6},{6,7},{8,9},{9,10},{10,11},{12,13},{... | collective-permute-start | bytes 76808 | tf_op jit(solution)/shard_map/ppermute | solution.py:23
  33.6 6.4 %collective-permute-start.5 = (f32[5,8,40,4]{2,1,3,0:T(8,128)S(1)}, f32[5,8,40,4]{2,1,3,0:T(8,128)}, u32[]{:S(2)}, u32[]{:S(2)}) collective-permute-start(f32[5,8,40,4]{2,1,3,0:T(8,128)S(1)} %copy.29), channel_id=1, source_target_pairs={{1,0},{2,1},{3,2},{5,4},{6,5},{7,6},{9,8},{10,9},{11,10},{13,12},{... | collective-permute-start | bytes 76808 | tf_op jit(solution)/shard_map/ppermute | solution.py:25
  38.2 4.1 %copy-start.2 = (f32[5,8,32,128]{3,1,2,0:T(8,128)S(1)}, f32[5,8,32,128]{3,1,2,0:T(8,128)}, u32[]{:S(2)}) copy-start(f32[5,8,32,128]{3,1,2,0:T(8,128)} %fusion.6) | copy-start | bytes 1966084
